TPU v7x, 32 devices: a whole 2x2x4 slice. The times are simulated.
32 devices in a mesh: leaf: 4 (over z), front: 8 (over y, x, core).
Axes of the slice: x: 2, y: 2, z: 4, core: 2. Of those that a mesh axis runs over, the one named last changes fastest.
Arguments:
- rhs_leaf: float32 [4, 2048, 64], P('leaf', 'front'), may hold values from -2.4 to 2.4
- diag_inv: bfloat16 [4, 8, 256, 256], P('leaf', 'front'), as said below
- sub_block: bfloat16 [4, 8, 256, 256], P('leaf', 'front'), as said below
- coupling: bfloat16 [4, 256, 2048], P('leaf', None, 'front'), may hold values from -0.25 to 0.25
- update_rows: int32 [4, 256], P('leaf'), may hold values from 0 to 1023, as said below
- rhs_sep: float32 [1024, 64], P('leaf'), may hold values from -6 to 6
- sep_inv: bfloat16 [1024, 1024], P('front', 'leaf'), as said below
Outputs:
- leaf_solution: float32 [4, 2048, 64], P('leaf', 'front')
- separator_solution: float32 [1024, 64], P('leaf')
Inputs may be any that keep to these rules, and one draw needn't show every extreme that they name: `update_rows`: within a group the 256 indices are distinct and increasing, and include the first and the last separator row. `diag_inv`: each 256 x 256 block is lower triangular. `sub_block`: each 256 x 256 block is lower triangular. `sep_inv`: lower triangular.
All inputs are finite; a program needn't handle non-finite values.
Results may differ from a plain program's by a relative error of at most 0.0003.
Values may be sent and summed in bfloat16 or wider, within the bound.
A program may use at most 64 MiB of HBM per device.

v0:
```python
import jax
import jax.numpy as jnp
from jax import lax
from jax.sharding import PartitionSpec as P

S = 1024
PRECISE = lax.Precision.HIGHEST


def carried_in(value, axis, join, neutral, backward):
    count, mine = (lax.axis_size(axis), lax.axis_index(axis))
    pieces = jax.tree.map(lambda part: lax.all_gather(part, axis), value)
    if backward:
        pieces = jax.tree.map(lambda part: part[::-1], pieces)
        mine = count - 1 - mine
    total = jax.tree.map(
        lambda part, zero: jnp.full_like(part, 0) + jnp.asarray(zero, part.dtype), value, neutral
    )

    def step(position, total):
        longer = join(total, jax.tree.map(lambda part: part[position], pieces))
        return jax.tree.map(lambda new, old: jnp.where(position < mine, new, old), longer, total)

    return lax.fori_loop(0, count - 1, step, total)


def shifted_2(value, axis, steps):
    count = lax.axis_size(axis)
    initial, last = (max(0, -steps), min(count, count - steps))
    return lax.ppermute(value, axis, [(source, source + steps) for source in range(initial, last)])


def product(left, right):
    return jnp.matmul(left, right, precision=PRECISE)


def narrow_product(left, right):
    return jnp.dot(left, right, preferred_element_type=jnp.float32)


def compose(earlier, later):
    return (product(later[0], earlier[0]), product(later[0], earlier[1]) + later[1])


def apply_maps(state, inputs):
    step_map, offset = inputs
    value = product(step_map, state) + offset
    return (value, value)


def forward_maps(carry, inputs):
    inverse, couple, right = inputs
    step_map = -narrow_product(inverse, couple)
    offset = product(inverse.astype(jnp.float32), right)
    mapped, shifted = carry
    return ((product(step_map, mapped), product(step_map, shifted) + offset), (step_map, offset))


def backward_maps(carry, inputs):
    inverse, couple, right = inputs
    step_map = -narrow_product(couple, inverse).T
    offset = product(inverse.astype(jnp.float32).T, right)
    mapped, shifted = carry
    return ((product(step_map, mapped), product(step_map, shifted) + offset), (step_map, offset))


def shards(rhs_leaf, diag_inv, sub_block, coupling, update_rows, rhs_sep, sep_inv):
    count = diag_inv.shape[1]
    width = diag_inv.shape[2]
    columns = rhs_leaf.shape[2]
    identity_w = jnp.eye(width, dtype=jnp.float32)
    zero_state = jnp.zeros((width, columns), jnp.float32)
    blocks = rhs_leaf[0].reshape(count, width, columns)
    (whole_map, whole_shift), (maps_fwd, offsets_fwd) = lax.scan(
        forward_maps, (identity_w, zero_state), (diag_inv[0], sub_block[0], blocks)
    )
    entering = carried_in(
        (whole_map, whole_shift), "front", compose, (identity_w, zero_state), False
    )
    _, solved_fwd = lax.scan(apply_maps, entering[1], (maps_fwd, offsets_fwd))
    forward_local = solved_fwd.reshape(count * width, columns)
    coupling_full = coupling[0].astype(jnp.float32)
    group_rows = product(coupling_full, forward_local)
    selector = (jnp.arange(S)[:, None] == update_rows[0][None, :]).astype(jnp.float32)
    update_term = product(selector, group_rows)
    gathered = lax.all_gather(sep_inv, "leaf", axis=1, tiled=True)
    whole_inv = lax.all_gather(gathered, "front", axis=0, tiled=True).astype(jnp.float32)
    rows_here = rhs_sep.shape[0]
    placed = lax.dynamic_update_slice_in_dim(
        jnp.zeros((S, columns), jnp.float32), rhs_sep, lax.axis_index("leaf") * rows_here, 0
    )
    leader = (lax.axis_index("front") == 0).astype(jnp.float32)
    reduced = lax.psum(leader * placed - update_term, ("leaf", "front"))
    sep_forward = product(whole_inv, reduced)
    solution_all = product(whole_inv.T, sep_forward)
    solution_sep = lax.dynamic_slice_in_dim(
        solution_all, lax.axis_index("leaf") * rows_here, rows_here, 0
    )
    selected_entries = product(selector.T, solution_all)
    adjusted = forward_local - product(coupling_full.T, selected_entries)
    next_first = shifted_2(sub_block[0, 0], "front", -1)
    following = jnp.concatenate([sub_block[0, 1:], next_first[None]], axis=0)
    adjusted_blocks = adjusted.reshape(count, width, columns)
    (back_map, back_shift), (maps_back, offsets_back) = lax.scan(
        backward_maps,
        (identity_w, zero_state),
        (diag_inv[0], following, adjusted_blocks),
        reverse=True,
    )
    arriving = carried_in((back_map, back_shift), "front", compose, (identity_w, zero_state), True)
    _, solved_back = lax.scan(apply_maps, arriving[1], (maps_back, offsets_back), reverse=True)
    return (solved_back, solution_sep)


def solution(mesh):
    return jax.shard_map(
        shards,
        mesh=mesh,
        in_specs=(
            P("leaf", "front", None),
            P("leaf", "front", None, None),
            P("leaf", "front", None, None),
            P("leaf", None, "front"),
            P("leaf", None),
            P("leaf", None),
            P("front", "leaf"),
        ),
        out_specs=(P("leaf", "front", None), P("leaf", None)),
        check_vma=False,
    )
```

profile of v0, /device:TPU:0, one launch (start us, length us, event | category | flops | bytes accessed | tf_op | source)
XLA Modules:
  0.0 245.7 jit_solution(13124845417316200062)
XLA Ops:
  8.1 1.1 convolution_negate_fusion
  10.2 1.3 collective-permute-start
  11.5 17.9 %all_gather.36 = bf16[128,1024]{1,0:T(8,128)(2,1)} all-gather(bf16[128,256]{1,0:T(8,128)(2,1)} %param.17), channel_id=1, replica_groups=mesh['leaf'=4,'front'=8] {'leaf'}, dimensions={1}, use_global_device_ids=true | all-gather | bytes 327680 | tf_op jit(solution)/shard_map/all_gather | solution.py:86
  29.5 1.1 fusion.29
  31.0 11.6 %all-gather.2 = f32[2048,64]{0,1:T(8,128)S(1)} all-gather(f32[256,64]{0,1:T(8,128)S(1)} %convolution_add_fusion.4), channel_id=4, replica_groups=mesh['leaf'=4,'front'=8] {'front'}, dimensions={0}, use_global_device_ids=true | all-gather | bytes 589824 | tf_op jit(solution)/shard_map/all_gather | solution.py:12
  43.2 10.0 %while.18 = (s32[]{:T(128)}, f32[256,64]{0,1:T(8,128)S(1)}, s32[]{:T(128)}, f32[8,256,256]{2,1,0:T(8,128)}, f32[8,256,64]{1,0,2:T(8,128)S(1)}, /*index=5*/s32[]{:T(128)}, s32[]{:T(128)}) while((s32[]{:T(128)}, f32[256,64]{0,1:T(8,128)S(1)}, s32[]{:T(128)}, f32[8,256,256]{2,1,0:T(8,128)}, f32[8,256,64]{1,0,2:T(8,128)S(1)}, ...), condition=%wide.region_1.2_spmd.clone, body=%wide.region_0.1_spmd.clone.sunk | while | flops 50397188 | bytes 788587 | solution.py:24
  43.3 1.3 fusion.67
  44.7 1.3 fusion.67
  46.1 1.3 fusion.67
  47.5 1.3 fusion.67
  48.9 1.3 fusion.67
  50.4 1.3 fusion.67
  51.8 1.3 fusion.67
  53.8 1.3 convolution_subtract_fusion
  55.2 1.0 fusion.24
  56.2 16.5 %all-gather.8.cloned.1.call-done = bf16[1024,1024]{1,0:T(8,128)(2,1)} async-done(((bf16[128,1024]{1,0:T(8,128)(2,1)}), bf16[1024,1024]{1,0:T(8,128)(2,1)}) %all-gather.8.cloned.1.call-update) | async-done | bytes 2097168 | tf_op jit(solution)/shard_map/all_gather | solution.py:87
  72.7 130.5 %all-reduce.2.cloned.1.call-done = f32[1024,64]{0,1:T(8,128)} async-done(((f32[1024,64]{0,1:T(8,128)}), f32[1024,64]{0,1:T(8,128)}) %all-reduce.2.cloned.1.call-update) | async-done | bytes 262160 | tf_op jit(solution)/shard_map/psum | solution.py:93
  203.3 3.7 %fusion.39 = f32[64,1024]{1,0:T(8,128)S(1)} fusion(f32[1024,64]{0,1:T(8,128)} %all-reduce.2.cloned.1.call-done, bf16[1024,1024]{1,0:T(8,128)(2,1)} %all-gather.8.cloned.1.call-done), kind=kOutput, calls=%fused_computation.56 | convolution fusion | flops 805306368 | bytes 2621440 | tf_op jit(solution)/shard_map/dot_general | solution.py:34
  207.0 1.2 fusion.40
  209.8 10.4 %all-gather.3 = f32[2048,64]{0,1:T(8,128)S(1)} all-gather(f32[256,64]{0,1:T(8,128)S(1)} %convolution_add_fusion.5), channel_id=5, replica_groups=mesh['leaf'=4,'front'=8] {'front'}, dimensions={0}, use_global_device_ids=true | all-gather | bytes 589824 | tf_op jit(solution)/shard_map/all_gather | solution.py:12
  221.0 12.4 %all-gather.10.cloned.1.call-done = f32[2048,256]{1,0:T(8,128)} async-done(((f32[256,256]{1,0:T(8,128)}), f32[2048,256]{1,0:T(8,128)}) %all-gather.10.cloned.1.call-update) | async-done | bytes 2097168 | tf_op jit(solution)/shard_map/all_gather | solution.py:12
  233.4 1.8 rev.6
  235.2 2.9 %while.19 = (s32[]{:T(128)}, f32[256,64]{0,1:T(8,128)S(1)}, s32[]{:T(128)}, f32[8,256,256]{2,1,0:T(8,128)S(1)}, f32[8,256,64]{1,2,0:T(8,128)S(1)}, /*index=5*/s32[]{:T(128)}, s32[]{:T(128)}) while((s32[]{:T(128)}, f32[256,64]{0,1:T(8,128)S(1)}, s32[]{:T(128)}, f32[8,256,256]{2,1,0:T(8,128)S(1)}, f32[8,256,64]{1,2,0:T(8,128)S(1)}, ...), condition=%wide.region_4.5_spmd.clone, body=%wide.region_3.4_spmd.clone.sunk | while | flops 50397188 | bytes 658023 | solution.py:24
  238.1 1.0 fusion.17
  (65 shorter events, 8.9 us)
Async XLA Ops:
  7.2 0.9 copy-start
  7.2 35.9 %all-gather.12.cloned.1.call-start = ((), (), s32[]{:S(2)}) async-start(), calls=%async_computation.3 | async-start | bytes 2359296 | tf_op jit(solution)/shard_map/all_gather | solution.py:12
  9.2 33.7 %copy-start.3 = (f32[256,64]{0,1:T(8,128)S(1)}, f32[256,64]{0,1:T(8,128)}, u32[]{:S(2)}) copy-start(f32[256,64]{0,1:T(8,128)} %param.16) | copy-start | bytes 196612
  10.2 62.6 %all-gather.8.cloned.1.call-start = ((), (), s32[]{:S(2)}) async-start(), calls=%async_computation.1 | async-start | bytes 2359296 | tf_op jit(solution)/shard_map/all_gather | solution.py:87
  10.2 32.6 %collective-permute-start = (bf16[256,256]{1,0:T(8,128)(2,1)}, bf16[256,256]{1,0:T(8,128)(2,1)S(1)}, u32[]{:S(2)}, u32[]{:S(2)}) collective-permute-start(bf16[256,256]{1,0:T(8,128)(2,1)} %bitcast.85), channel_id=1, source_target_pairs={{1,0},{2,1},{3,2},{4,3},{5,4},{6,5},{7,6},{9,8},{10,9},{11,10},{12... | collective-permute-start | bytes 393224 | tf_op jit(solution)/shard_map/ppermute | solution.py:30
  29.5 173.8 %all-reduce.2.cloned.1.call-start = ((), (), s32[]{:S(2)}) async-start(), calls=%async_computation | async-start | bytes 524288 | tf_op jit(solution)/shard_map/psum | solution.py:93
  43.1 10.4 %copy-start.2 = (bf16[1,256,256]{2,1,0:T(8,128)(2,1)S(1)}, bf16[1,256,256]{2,1,0:T(8,128)(2,1)}, u32[]{:S(2)}) copy-start(bf16[1,256,256]{2,1,0:T(8,128)(2,1)} %param.14) | copy-start | bytes 393220
  43.1 10.6 %copy-start.4 = (s32[1,256]{1,0:T(1,128)S(1)}, s32[1,256]{1,0:T(1,128)}, u32[]{:S(2)}) copy-start(s32[1,256]{1,0:T(1,128)} %param.15) | copy-start | bytes 3076
  55.2 178.2 %all-gather.10.cloned.1.call-start = ((), (), s32[]{:S(2)}) async-start(), calls=%async_computation.2 | async-start | bytes 2359296 | tf_op jit(solution)/shard_map/all_gather | solution.py:12
  72.7 134.2 %copy-start.1 = (bf16[1024,1024]{1,0:T(8,128)(2,1)S(1)}, bf16[1024,1024]{1,0:T(8,128)(2,1)}, u32[]{:S(2)}) copy-start(bf16[1024,1024]{1,0:T(8,128)(2,1)} %all-gather.8.cloned.1.call-done) | copy-start | bytes 6291460
Sparse Core Ops, SparseCore 0:
  10.3 31.7 all-gather.11
  44.0 28.7 all-gather.7
  78.2 124.9 all-reduce.1
  205.0 28.3 all-gather.9
where the time goes:
time: 246 us
  waiting for transfers between devices  160 us (65%)
  blocking collectives  40 us (16%)
  matrix products  26.2 us (11%)
  between operations  14 us (6%)
  local copies, waits for them, and re-layouts  4.04 us (2%)
    psum x1, waiting for transfers between devices, shards(): reduced = lax.psum(leader * placed - update_term, ('leaf', 'front'))  131 us
    dot_general x28, matrix products, product(): return jnp.matmul(left, right, precision=PRECISE)  24.9 us
    all_gather x2, blocking collectives, carried_in(): pieces = jax.tree.map(lambda part: lax.all_gather(part, axis), value)  22 us
    all_gather x1, blocking collectives, shards(): gathered = lax.all_gather(sep_inv, 'leaf', axis=1, tiled=True)  17.9 us
    all_gather x1, waiting for transfers between devices, shards(): lax.all_gather(gathered, 'front', axis=0, tiled=True).astype(jnp.float32)  16.5 us
    all_gather x2, waiting for transfers between devices, carried_in(): pieces = jax.tree.map(lambda part: lax.all_gather(part, axis), value)  12.5 us
  transfers between devices with their start and end apart: 5, of which 3 were waited for; matrix products, arithmetic and copies ran while one was open for 9% of the time, Pallas kernels for 0%

commit v1 on v0

--- a/solution.py
+++ b/solution.py
@@ -5,6 +5,12 @@
 
 S = 1024
 PRECISE = lax.Precision.HIGHEST
+
+
+def gather_and_add(x, axis):
+    parts = lax.all_gather(x, axis, axis=0, tiled=False)
+    total = parts.sum(axis=0)
+    return total
 
 
 def carried_in(value, axis, join, neutral, backward):
@@ -90,7 +96,7 @@
         jnp.zeros((S, columns), jnp.float32), rhs_sep, lax.axis_index("leaf") * rows_here, 0
     )
     leader = (lax.axis_index("front") == 0).astype(jnp.float32)
-    reduced = lax.psum(leader * placed - update_term, ("leaf", "front"))
+    reduced = gather_and_add(leader * placed - update_term, ("leaf", "front"))
     sep_forward = product(whole_inv, reduced)
     solution_all = product(whole_inv.T, sep_forward)
     solution_sep = lax.dynamic_slice_in_dim(

time: 246 us -> 215 us (0.87)
  waiting for transfers between devices: 160 us -> 113 us
  local copies, waits for them, and re-layouts: 4.04 us -> 13 us
  matrix products: 26.2 us -> 31.4 us
    psum x1 -> x0, waiting for transfers between devices: 131 us -> none  [shards(): reduced = lax.psum(leader * placed - update_term, ('leaf', 'front'))]
    all_gather x0 -> x1, waiting for transfers between devices: none -> 79 us  [gather_and_add(): parts = lax.all_gather(x, axis, axis=0, tiled=False)]
    unnamed x11 -> x16, local copies, waits for them, and re-layouts: 1.04 us -> 9.14 us
    dot_general x28, matrix products: 24.9 us -> 30.1 us  [product(): return jnp.matmul(left, right, precision=PRECISE)]
    all_gather x1, blocking collectives: 17.9 us -> 14.8 us  [shards(): gathered = lax.all_gather(sep_inv, 'leaf', axis=1, tiled=True)]
    all_gather x2, blocking collectives: 22 us -> 24.8 us  [carried_in(): pieces = jax.tree.map(lambda part: lax.all_gather(part, axis), value)]
  transfers between devices with their start and end apart: 5 -> 5, of which waited for: 3 -> 5; matrix products, arithmetic and copies ran while one was open for 9% -> 12% of each run, Pallas kernels for 0% -> 0%
where the time goes in v1:
time: 215 us
  waiting for transfers between devices  113 us (53%)
  blocking collectives  39.5 us (18%)
  matrix products  31.4 us (15%)
  between operations  14 us (7%)
  local copies, waits for them, and re-layouts  13 us (6%)
    all_gather x1, waiting for transfers between devices, gather_and_add(): parts = lax.all_gather(x, axis, axis=0, tiled=False)  79 us
    dot_general x28, matrix products, product(): return jnp.matmul(left, right, precision=PRECISE)  30.1 us
    all_gather x2, blocking collectives, carried_in(): pieces = jax.tree.map(lambda part: lax.all_gather(part, axis), value)  24.8 us
    all_gather x1, waiting for transfers between devices, shards(): lax.all_gather(gathered, 'front', axis=0, tiled=True).astype(jnp.float32)  18.6 us
    all_gather x1, blocking collectives, shards(): gathered = lax.all_gather(sep_inv, 'leaf', axis=1, tiled=True)  14.8 us
    all_gather x2, waiting for transfers between devices, carried_in(): pieces = jax.tree.map(lambda part: lax.all_gather(part, axis), value)  13.7 us
    unnamed x16, local copies, waits for them, and re-layouts  9.14 us
  transfers between devices with their start and end apart: 5, of which 5 were waited for; matrix products, arithmetic and copies ran while one was open for 12% of the time, Pallas kernels for 0%

profile of v1, /device:TPU:0, one launch (start us, length us, event | category | flops | bytes accessed | tf_op | source)
XLA Modules:
  0.0 214.6 jit_solution(17451194447428540216)
XLA Ops:
  10.2 1.3 collective-permute-start
  11.5 2.2 %collective-permute-done = bf16[256,256]{1,0:T(8,128)(2,1)S(1)} collective-permute-done((bf16[256,256]{1,0:T(8,128)(2,1)}, bf16[256,256]{1,0:T(8,128)(2,1)S(1)}, u32[]{:S(2)}, u32[]{:S(2)}) %collective-permute-start) | collective-permute-done | bytes 131104 | tf_op jit(solution)/shard_map/ppermute | solution.py:36
  15.7 14.9 %all-gather.2 = f32[2048,64]{0,1:T(8,128)S(1)} all-gather(f32[256,64]{0,1:T(8,128)S(1)} %convolution_add_fusion.4), channel_id=4, replica_groups=mesh['leaf'=4,'front'=8] {'front'}, dimensions={0}, use_global_device_ids=true | all-gather | bytes 589824 | tf_op jit(solution)/shard_map/all_gather | solution.py:18
  30.9 10.8 %all-gather.14.cloned.1.call-done = f32[2048,256]{1,0:T(8,128)} async-done(((f32[256,256]{1,0:T(8,128)}), f32[2048,256]{1,0:T(8,128)}) %all-gather.14.cloned.1.call-update) | async-done | bytes 2097168 | tf_op jit(solution)/shard_map/all_gather | solution.py:18
  41.6 10.0 %while.18 = (s32[]{:T(128)}, f32[256,64]{0,1:T(8,128)S(1)}, s32[]{:T(128)}, f32[8,256,256]{2,1,0:T(8,128)}, f32[8,256,64]{1,0,2:T(8,128)S(1)}, /*index=5*/s32[]{:T(128)}, s32[]{:T(128)}) while((s32[]{:T(128)}, f32[256,64]{0,1:T(8,128)S(1)}, s32[]{:T(128)}, f32[8,256,256]{2,1,0:T(8,128)}, f32[8,256,64]{1,0,2:T(8,128)S(1)}, ...), condition=%wide.region_1.2_spmd.clone, body=%wide.region_0.1_spmd.clone.sunk | while | flops 50397188 | bytes 788579 | solution.py:30
  41.7 1.4 fusion.67
  43.2 1.3 fusion.67
  44.6 1.3 fusion.67
  46.0 1.3 fusion.67
  47.4 1.3 fusion.67
  48.9 1.3 fusion.67
  50.3 1.3 fusion.67
  52.3 1.4 convolution_subtract_fusion
  53.7 14.8 %all_gather.44 = bf16[128,1024]{1,0:T(8,128)(2,1)} all-gather(bf16[128,256]{1,0:T(8,128)(2,1)S(1)} %copy-done.3), channel_id=1, replica_groups=mesh['leaf'=4,'front'=8] {'leaf'}, dimensions={1}, use_global_device_ids=true | all-gather | bytes 327680 | tf_op jit(solution)/shard_map/all_gather | solution.py:92
  68.6 2.9 %all-gather.12.cloned.1.call-done = f32[2048,256]{1,0:T(8,128)} async-done(((f32[256,256]{1,0:T(8,128)}), f32[2048,256]{1,0:T(8,128)}) %all-gather.12.cloned.1.call-update) | async-done | bytes 2097168 | tf_op jit(solution)/shard_map/all_gather | solution.py:18
  71.4 1.8 rev.6
  73.3 79.0 %all-gather.16.cloned.1.call-done = f32[32768,64]{0,1:T(8,128)} async-done(((f32[1024,64]{0,1:T(8,128)}), f32[32768,64]{0,1:T(8,128)}) %all-gather.16.cloned.1.call-update) | async-done | bytes 8388624 | tf_op jit(solution)/shard_map/all_gather | solution.py:11
  152.2 8.1 %copy.16 = f32[8,8,32,1024]{3,2,1,0:T(8,128)S(1)} copy(f32[8,8,32,1024]{3,1,2,0:T(8,128)} %bitcast.84) | data formatting | bytes 16777216
  160.4 1.5 bitcast_reduce_fusion
  161.8 18.6 %all-gather.10.cloned.1.call-done = bf16[1024,1024]{1,0:T(8,128)(2,1)} async-done(((bf16[128,1024]{1,0:T(8,128)(2,1)}), bf16[1024,1024]{1,0:T(8,128)(2,1)}) %all-gather.10.cloned.1.call-update) | async-done | bytes 2097168 | tf_op jit(solution)/shard_map/all_gather | solution.py:93
  180.4 3.8 %fusion.39 = f32[64,1024]{1,0:T(8,128)S(1)} fusion(f32[1024,64]{0,1:T(8,128)S(1)} %bitcast_reduce_fusion, bf16[1024,1024]{1,0:T(8,128)(2,1)} %all-gather.10.cloned.1.call-done), kind=kOutput, calls=%fused_computation.57 | convolution fusion | flops 805306368 | bytes 2621440 | tf_op jit(solution)/shard_map/dot_general | solution.py:40
  187.6 9.8 %all-gather.4 = f32[2048,64]{0,1:T(8,128)S(1)} all-gather(f32[256,64]{0,1:T(8,128)S(1)} %convolution_add_fusion.5), channel_id=6, replica_groups=mesh['leaf'=4,'front'=8] {'front'}, dimensions={0}, use_global_device_ids=true | all-gather | bytes 589824 | tf_op jit(solution)/shard_map/all_gather | solution.py:18
  198.3 8.8 %while.19 = (s32[]{:T(128)}, f32[256,64]{0,1:T(8,128)S(1)}, s32[]{:T(128)}, f32[8,256,256]{2,1,0:T(8,128)S(1)}, f32[8,256,64]{1,2,0:T(8,128)}, /*index=5*/s32[]{:T(128)}, s32[]{:T(128)}) while((s32[]{:T(128)}, f32[256,64]{0,1:T(8,128)S(1)}, s32[]{:T(128)}, f32[8,256,256]{2,1,0:T(8,128)S(1)}, f32[8,256,64]{1,2,0:T(8,128)}, ...), condition=%wide.region_4.5_spmd.clone, body=%wide.region_3.4_spmd.clone.sunk | while | flops 50397188 | bytes 658015 | solution.py:30
  199.6 1.2 fusion.70
  (71 shorter events, 19.0 us)
Async XLA Ops:
  7.2 0.9 copy-start
  7.2 7.8 %copy-start.5 = (f32[1,256,64]{1,2,0:T(8,128)S(1)}, f32[1,256,64]{1,2,0:T(8,128)}, u32[]{:S(2)}) copy-start(f32[1,256,64]{1,2,0:T(8,128)} %param.11) | copy-start | bytes 196612
  7.2 34.4 %all-gather.14.cloned.1.call-start = ((), (), s32[]{:S(2)}) async-start(), calls=%async_computation.2 | async-start | bytes 2359296 | tf_op jit(solution)/shard_map/all_gather | solution.py:18
  10.2 20.7 %copy-start.4 = (f32[256,64]{0,1:T(8,128)S(1)}, f32[256,64]{0,1:T(8,128)}, u32[]{:S(2)}) copy-start(f32[256,64]{0,1:T(8,128)} %param.16) | copy-start | bytes 196612
  10.2 61.3 %all-gather.12.cloned.1.call-start = ((), (), s32[]{:S(2)}) async-start(), calls=%async_computation.1 | async-start | bytes 2359296 | tf_op jit(solution)/shard_map/all_gather | solution.py:18
  10.2 3.5 %collective-permute-start = (bf16[256,256]{1,0:T(8,128)(2,1)}, bf16[256,256]{1,0:T(8,128)(2,1)S(1)}, u32[]{:S(2)}, u32[]{:S(2)}) collective-permute-start(bf16[256,256]{1,0:T(8,128)(2,1)} %bitcast.91), channel_id=1, source_target_pairs={{1,0},{2,1},{3,2},{4,3},{5,4},{6,5},{7,6},{9,8},{10,9},{11,10},{12... | collective-permute-start | bytes 393224 | tf_op jit(solution)/shard_map/ppermute | solution.py:36
  15.0 137.3 %all-gather.16.cloned.1.call-start = ((), (), s32[]{:S(2)}) async-start(), calls=%async_computation.3 | async-start | bytes 8650752 | tf_op jit(solution)/shard_map/all_gather | solution.py:11
  41.6 10.4 %copy-start.2 = (bf16[1,256,256]{2,1,0:T(8,128)(2,1)S(1)}, bf16[1,256,256]{2,1,0:T(8,128)(2,1)}, u32[]{:S(2)}) copy-start(bf16[1,256,256]{2,1,0:T(8,128)(2,1)} %param.14) | copy-start | bytes 393220
  41.6 10.7 %copy-start.6 = (s32[1,256]{1,0:T(1,128)S(1)}, s32[1,256]{1,0:T(1,128)}, u32[]{:S(2)}) copy-start(s32[1,256]{1,0:T(1,128)} %param.15) | copy-start | bytes 3076
  41.6 12.1 %copy-start.3 = (bf16[128,256]{1,0:T(8,128)(2,1)S(1)}, bf16[128,256]{1,0:T(8,128)(2,1)}, u32[]{:S(2)}) copy-start(bf16[128,256]{1,0:T(8,128)(2,1)} %param.17) | copy-start | bytes 196612
  53.7 126.7 %all-gather.10.cloned.1.call-start = ((), (), s32[]{:S(2)}) async-start(), calls=%async_computation | async-start | bytes 2359296 | tf_op jit(solution)/shard_map/all_gather | solution.py:93
  180.4 3.8 %copy-start.1 = (bf16[1024,1024]{1,0:T(8,128)(2,1)S(1)}, bf16[1024,1024]{1,0:T(8,128)(2,1)}, u32[]{:S(2)}) copy-start(bf16[1024,1024]{1,0:T(8,128)(2,1)} %all-gather.10.cloned.1.call-done) | copy-start | bytes 6291460
Sparse Core Ops, SparseCore 0:
  10.3 31.2 all-gather.13
  43.5 27.8 all-gather.11
  74.4 77.8 all-gather.15
  154.0 26.3 all-gather.9
